TPU v7x, 32 devices: a whole 2x2x4 slice. The times are simulated.
32 devices in a mesh: feed: 8 (over y, x, core), tm: 4 (over z).
Axes of the slice: x: 2, y: 2, z: 4, core: 2. Of those that a mesh axis runs over, the one named last changes fastest.
Arguments:
- voltages: bfloat16 [256, 1048576], P('feed', 'tm'), may hold values from -12 to 12
- filter_taps: float32 [4, 1024], replicated, may hold values from -1 to 1
- delays: float32 [256], P('feed'), may hold values from -64 to 64
- channel_flags: int32 [512], P('feed'), may hold values from 0 to 1, as said below
Outputs:
- visibilities: float32 [512, 256, 256], P(('feed', 'tm'))
Inputs may be any that keep to these rules, and one draw needn't show every extreme that they name: `channel_flags`: channel c belongs to owner c // 64; every owner keeps between 16 and 64 of its channels, and in every draw some owner keeps all of them.
All inputs are finite; a program needn't handle non-finite values.
Results may differ from a plain program's by a relative error of at most 0.0011.
Values may be sent and summed in bfloat16 or wider, within the bound.
A program may use at most 192 MiB of HBM per device.

v0:
```python
import math
import jax
import jax.numpy as jnp
from jax import lax
from jax.sharding import PartitionSpec as P


def passed_along(block, axis, distance):
    devices = range(lax.axis_size(axis))
    route = [(i - distance, i) for i in devices if i - distance in devices]
    return lax.ppermute(block, axis, route)


def build_table(fft_length):
    channels = jnp.arange(fft_length // 2, dtype=jnp.int32)
    samples = jnp.arange(fft_length, dtype=jnp.int32)
    product = channels[:, None] * samples[None, :] % fft_length
    angles = product.astype(jnp.float32) * (2.0 * math.pi / fft_length)
    return jnp.stack([jnp.cos(angles), -jnp.sin(angles)], axis=1).astype(jnp.bfloat16)


def rotate_phase(real_part, imag_part, channels, delay_values, fft_length):
    angles = 2.0 * math.pi / fft_length * channels * delay_values
    cosine = jnp.cos(angles)
    sine_part = jnp.sin(angles)
    factor = 1.0 / math.sqrt(fft_length)
    return (
        (real_part * cosine + imag_part * sine_part) * factor,
        (imag_part * cosine - real_part * sine_part) * factor,
    )


def gram_blocks(turned, local_frame_count, frame_total):
    count_here, inputs_all, columns = turned.shape
    split = turned.reshape(
        count_here, inputs_all, columns // (2 * local_frame_count), 2, local_frame_count
    )
    real_half = split[:, :, :, 0].reshape(count_here, inputs_all, columns // 2)
    imag_half = split[:, :, :, 1].reshape(count_here, inputs_all, columns // 2)
    block_rows = min(128, inputs_all)
    column_index = jnp.arange(inputs_all)[None, :]
    row_blocks = []
    for first in range(0, inputs_all, block_rows):
        last = first + block_rows
        upper = jnp.einsum(
            "cik,cjk->cij",
            turned[:, first:last],
            turned[:, first:],
            preferred_element_type=jnp.float32,
        )
        lower = jnp.einsum(
            "cik,cjk->cij",
            imag_half[:, first:last],
            real_half[:, :last],
            preferred_element_type=jnp.float32,
        )
        lower = lower - jnp.einsum(
            "cik,cjk->cij",
            real_half[:, first:last],
            imag_half[:, :last],
            preferred_element_type=jnp.float32,
        )
        upper_full = jnp.pad(upper, ((0, 0), (0, 0), (first, 0)))
        lower_full = jnp.pad(lower, ((0, 0), (0, 0), (0, inputs_all - last)))
        row_index = jnp.arange(first, last)[:, None]
        row_blocks.append(jnp.where(row_index <= column_index, upper_full, lower_full))
    return jnp.concatenate(row_blocks, axis=1) / frame_total


def on_device(voltages, filter_taps, delays, channel_flags):
    inputs_here, sample_count = voltages.shape
    tap_count, fft_length = filter_taps.shape
    local_frame_count = sample_count // fft_length
    frames = voltages.reshape(inputs_here, local_frame_count, fft_length)
    history = passed_along(frames[:, local_frame_count - (tap_count - 1) :, :], "tm", 1)
    extended = jnp.concatenate([history, frames], axis=1).astype(jnp.float32)
    filtered = filter_taps[0] * extended[:, tap_count - 1 : tap_count - 1 + local_frame_count]
    for tap_index in range(1, tap_count):
        offset = tap_count - 1 - tap_index
        filtered = (
            filtered + filter_taps[tap_index] * extended[:, offset : offset + local_frame_count]
        )
    filtered = filtered.astype(jnp.bfloat16)
    dft_table = build_table(fft_length)
    raw_spectra = jnp.einsum(
        "cpn,isn->cips", dft_table, filtered, preferred_element_type=jnp.float32
    )
    channels = jnp.arange(fft_length // 2).astype(jnp.float32)[:, None, None]
    real_part, imag_part = rotate_phase(
        raw_spectra[:, :, 0], raw_spectra[:, :, 1], channels, delays[None, :, None], fft_length
    )
    spectra = jnp.concatenate([real_part, imag_part], axis=2).astype(jnp.bfloat16)
    time_devices = lax.axis_size("tm")
    frame_total = local_frame_count * time_devices
    channels_here = channel_flags.shape[0] // time_devices
    local_flags = lax.dynamic_slice_in_dim(
        channel_flags, lax.axis_index("tm") * channels_here, channels_here, 0
    )
    turned = lax.all_to_all(spectra, "feed", split_axis=0, concat_axis=1, tiled=True)
    visibility = lax.psum_scatter(
        gram_blocks(turned, local_frame_count, frame_total), "tm", scatter_dimension=0, tiled=True
    )
    return visibility * local_flags[:, None, None].astype(jnp.float32)


def solution(mesh):
    in_specs = (P("feed", "tm"), P(), P("feed"), P("feed"))
    out_specs = P(("feed", "tm"), None, None)
    return jax.shard_map(
        on_device, mesh=mesh, in_specs=in_specs, out_specs=out_specs, check_vma=False
    )
```

profile of v0, /device:TPU:0, one launch (start us, length us, event | category | flops | bytes accessed | tf_op | source)
XLA Modules:
  0.0 797.1 jit_solution(467650899731393742)
XLA Ops:
  6.5 0.0 copy-start.3
  6.5 0.0 copy-start.2
  6.5 15.4 %copy.23 = bf16[4,8,256,1024]{3,2,1,0:T(8,128)(2,1)S(1)} copy(bf16[4,8,256,1024]{3,1,2,0:T(8,128)(2,1)} %bitcast.67) | data formatting | bytes 33554432
  21.9 0.1 slice.79
  22.1 4.9 collective-permute-start
  27.0 8.5 %negate_convert_fusion = (bf16[512,1,1024]{2,0,1:T(8,128)(2,1)S(1)}, bf16[512,1,1024]{2,0,1:T(8,128)(2,1)S(1)}) fusion(), kind=kLoop, calls=%fused_computation.49 | loop fusion | flops 8912896 | bytes 2097152 | tf_op jit(solution)/shard_map/convert.3
  35.6 0.0 copy-done.3
  35.6 0.3 multiply_cosine_fusion
  35.9 0.0 copy-done.2
  35.9 0.0 collective-permute-done
  35.9 12.0 %maximum_convert_fusion = f32[32,259,1024]{2,1,0:T(8,128)} fusion(bf16[32,256,1024]{2,1,0:T(8,128)(2,1)S(1)} %bitcast.66, bf16[32,3,1024]{2,1,0:T(4,128)(2,1)S(1)} %collective-permute-done), kind=kLoop, calls=%fused_computation.8 | loop fusion | flops 33947648 | bytes 50921472 | tf_op jit(solution)/shard_map/convert_element_type | solution.py:76
  47.9 56.9 %fusion.10 = f32[512,32,2,256]{0,3,2,1:T(8,128)} fusion(f32[32,259,1024]{2,1,0:T(8,128)} %maximum_convert_fusion, f32[1024]{0:T(1024)S(1)} %bitcast.70, f32[1024]{0:T(1024)S(1)} %bitcast.71, f32[1024]{0:T(1024)S(1)} %bitcast.69, f32[1024]{0:T(1024)S(1)} %bitcast.68, bf16[512,1,1024]{2,0,1:T(8,128)(2,1)S(1)} %get-tuple-element.15, ...), kind=kOutput, calls=%fused_computation.20 | convolution fusion | flops 17251172352 | bytes 169885696 | tf_op jit(solution)/shard_map/cpn,isn->cips/dot_general | solution.py:85
  104.8 12.3 %multiply_convert_fusion.1 = (bf16[512,32,256]{0,2,1:T(8,128)(2,1)S(1)}, bf16[512,32,256]{0,2,1:T(8,128)(2,1)S(1)}) fusion(f32[512,32,2,256]{0,3,2,1:T(8,128)} %fusion.10, f32[512,32]{0,1:T(8,128)S(1)} %get-tuple-element.14, f32[512,32]{0,1:T(8,128)S(1)} %get-tuple-element.13), kind=kLoop, calls=%fused_computation.16 | loop fusion | flops 41943040 | bytes 50462720 | tf_op jit(solution)/shard_map/convert
  117.1 6.5 pad_maximum_fusion
  123.6 28.6 %copy.14 = bf16[512,32,512]{2,1,0:T(8,128)(2,1)} copy(bf16[512,32,512]{0,2,1:T(8,128)(2,1)} %pad_maximum_fusion) | data formatting | bytes 33554432 | tf_op jit(solution)/shard_map/concatenate | solution.py:92
  152.3 5.7 all-to-all-start
  158.0 0.2 reduce-scatter.2.cloned.1.call-start
  158.3 0.1 iota_compare_fusion
  158.4 183.6 %all-to-all-done = bf16[512,32,512]{2,1,0:T(8,128)(2,1)} async-done(((bf16[512,32,512]{2,1,0:T(8,128)(2,1)}), bf16[512,32,512]{2,1,0:T(8,128)(2,1)}, u32[]{:S(2)}, u32[]{:S(2)}) %all-to-all-start) | async-done | bytes 16777248 | tf_op jit(solution)/shard_map/all_to_all | solution.py:99
  341.9 14.1 %copy.15 = bf16[64,8,32,512]{3,2,1,0:T(8,128)(2,1)} copy(bf16[64,8,32,512]{3,2,0,1:T(8,128)(2,1)} %bitcast.11) | data formatting | bytes 33554432 | tf_op jit(solution)/shard_map/all_to_all | solution.py:99
  356.0 23.7 %reshape.151 = bf16[64,256,1,2,256]{4,3,1,0,2:T(2,128)(2,1)} reshape(bf16[64,8,32,512]{3,2,1,0:T(8,128)(2,1)} %copy.15) | data formatting | bytes 33554432 | tf_op jit(solution)/shard_map/reshape | solution.py:35
  379.7 32.4 %fusion.45 = (bf16[64,256,1,1,256]{4,3,1,0,2:T(2,128)(2,1)}, bf16[64,256,1,1,256]{4,3,1,0,2:T(2,128)(2,1)}) fusion(bf16[64,256,1,2,256]{4,3,1,0,2:T(2,128)(2,1)} %reshape.151), kind=kLoop, calls=%fused_computation.63 | loop fusion | bytes 33554432 | tf_op jit(solution)/shard_map/slice | solution.py:38
  412.2 8.9 %copy.26 = bf16[64,256,1,1,256]{4,1,0,3,2:T(8,128)(2,1)S(1)} copy(bf16[64,256,1,1,256]{4,3,1,0,2:T(2,128)(2,1)} %get-tuple-element.7) | data formatting | bytes 16777216
  421.1 0.0 copy-start
  421.1 11.9 %copy.27 = bf16[64,256,1,1,256]{4,1,0,3,2:T(8,128)(2,1)S(1)} copy(bf16[64,256,1,1,256]{4,3,1,0,2:T(2,128)(2,1)} %get-tuple-element.8) | data formatting | bytes 16777216
  433.1 0.0 copy-start.1
  433.1 3.2 copy-done.1
  436.3 3.3 fusion.21
  439.6 9.5 %fusion.17 = f32[64,128,256]{2,1,0:T(8,128)} fusion(bf16[64,256,256]{2,1,0:T(8,128)(2,1)} %bitcast.62, bf16[64,256,256]{2,1,0:T(8,128)(2,1)S(1)} %bitcast.58), kind=kOutput, calls=%fused_computation.29 | convolution fusion | flops 1073741824 | bytes 20971520 | tf_op jit(solution)/shard_map/cik,cjk->cij/dot_general | solution.py:57
  449.0 0.0 copy-done
  449.0 6.8 fusion.37
  455.9 10.1 %fusion.13 = f32[64,128,128]{2,1,0:T(8,128)} fusion(bf16[64,256,512]{2,1,0:T(8,128)(2,1)} %bitcast.55), kind=kOutput, calls=%fused_computation.21 | convolution fusion | flops 1073741824 | bytes 12582912 | tf_op jit(solution)/shard_map/cik,cjk->cij/dot_general | solution.py:45
  466.0 15.0 %pad_select_fusion = f32[64,128,256]{2,1,0:T(8,128)} fusion(f32[64,128,128]{2,1,0:T(8,128)} %fusion.37, pred[128,256]{1,0:T(8,128)(4,1)S(1)} %iota_compare_fusion.1, bf16[64,256,512]{2,1,0:T(8,128)(2,1)} %bitcast.56), kind=kOutput, calls=%fused_computation.28 | convolution fusion | flops 2149580800 | bytes 37781504 | tf_op jit(solution)/shard_map/cik,cjk->cij/dot_general | solution.py:45
  481.0 14.2 %subtract_select_fusion = f32[64,128,256]{2,1,0:T(8,128)} fusion(f32[64,128,256]{2,1,0:T(8,128)} %fusion.17, f32[64,128,128]{2,1,0:T(8,128)} %fusion.13, pred[128,256]{1,0:T(8,128)(4,1)S(1)} %iota_compare_fusion, bf16[64,256,256]{2,1,0:T(8,128)(2,1)} %bitcast.60, bf16[64,256,256]{2,1,0:T(8,128)(2,1)} %bitcast.64), kind=kOutput, calls=%fused_computation.27 | convolution fusion | flops 1077936128 | bytes 33587200 | tf_op jit(solution)/shard_map/cik,cjk->cij/dot_general | solution.py:51
  495.2 11.4 %maximum_multiply_fusion = f32[64,256,256]{2,1,0:T(8,128)} fusion(f32[64,128,256]{2,1,0:T(8,128)} %subtract_select_fusion, f32[64,128,256]{2,1,0:T(8,128)} %pad_select_fusion), kind=kLoop, calls=%fused_computation.12 | loop fusion | flops 8388608 | bytes 33554432 | tf_op jit(solution)/shard_map/div | solution.py:67
  506.7 0.0 copy-start.4
  506.7 0.0 reduce-scatter.2.cloned.1.call-update
  506.7 0.6 copy-done.4
  507.3 0.1 dynamic-slice_convert_fusion
  507.4 278.1 %reduce-scatter.2.cloned.1.call-done = f32[16,256,256]{2,1,0:T(8,128)} async-done(((f32[64,256,256]{2,1,0:T(8,128)}), f32[16,256,256]{2,1,0:T(8,128)}) %reduce-scatter.2.cloned.1.call-update) | async-done | bytes 4194320 | tf_op jit(solution)/shard_map/reduce_scatter | solution.py:100
  785.5 4.7 broadcast_multiply_fusion
  (4 shorter events, 0.0 us)
Async XLA Ops:
  6.5 29.0 %copy-start.3 = (f32[32]{0:T(128)S(1)}, f32[32]{0:T(128)}, u32[]{:S(2)}) copy-start(f32[32]{0:T(128)} %param.6) | copy-start | bytes 388
  6.5 29.3 %copy-start.2 = (f32[4,1024]{1,0:T(4,128)S(1)}, f32[4,1024]{1,0:T(4,128)}, u32[]{:S(2)}) copy-start(f32[4,1024]{1,0:T(4,128)} %param.5) | copy-start | bytes 49156
  22.1 13.8 %collective-permute-start = (bf16[32,3,1024]{2,1,0:T(4,128)(2,1)S(1)}, bf16[32,3,1024]{2,1,0:T(4,128)(2,1)S(1)}, u32[]{:S(2)}, u32[]{:S(2)}) collective-permute-start(bf16[32,3,1024]{2,1,0:T(4,128)(2,1)S(1)} %slice.79), channel_id=1, source_target_pairs={{0,1},{1,2},{2,3},{4,5},{5,6},{6,7},{8,9},{9,10},{10,11},{12,13},{... | collective-permute-start | bytes 589832 | tf_op jit(solution)/shard_map/ppermute | solution.py:11
  152.3 189.7 %all-to-all-start = ((bf16[512,32,512]{2,1,0:T(8,128)(2,1)}), bf16[512,32,512]{2,1,0:T(8,128)(2,1)}, u32[]{:S(2)}, u32[]{:S(2)}) async-start(bf16[512,32,512]{2,1,0:T(8,128)(2,1)} %copy.14), calls=%async_computation | async-start | bytes 33554432 | tf_op jit(solution)/shard_map/all_to_all | solution.py:99
  158.0 627.5 %reduce-scatter.2.cloned.1.call-start = ((), (), s32[]{:S(2)}) async-start(), calls=%async_computation.2 | async-start | bytes 20971520 | tf_op jit(solution)/shard_map/reduce_scatter | solution.py:100
  421.1 28.0 %copy-start = (bf16[64,256,1,1,256]{4,1,0,3,2:T(8,128)(2,1)}, bf16[64,256,1,1,256]{4,1,0,3,2:T(8,128)(2,1)S(1)}, u32[]{:S(2)}) copy-start(bf16[64,256,1,1,256]{4,1,0,3,2:T(8,128)(2,1)S(1)} %copy.26) | copy-start | bytes 25165828
  433.1 3.2 copy-start.1
  506.7 0.7 copy-start.4
Sparse Core Ops, SparseCore 0:
  506.8 278.6 reduce-scatter.1
where the time goes:
time: 799 us; the launch traced here: 797 us
  waiting for transfers between devices  462 us (58%)
  local copies, waits for them, and re-layouts  139 us (17%)
  matrix products  116 us (15%)
  other arithmetic  55.9 us (7%)
  between operations  13.6 us (2%)
  starting transfers between devices  10.9 us (1%)
    reduce_scatter x1, waiting for transfers between devices, on_device(): lax.psum_scatter(gram_blocks(turned, local_frame_count, frame_total), 'tm...  278 us
    all_to_all x1, waiting for transfers between devices, on_device(): lax.all_to_all(spectra, 'feed', split_axis=0, concat_axis=1, tiled=True)  184 us
    dot_general x1, matrix products, on_device(): jnp.einsum('cpn,isn->cips', dft_table, filtered, preferred_element_type=j...  56.9 us
    unnamed x13, local copies, waits for them, and re-layouts  40.1 us
    slice x1, local copies, waits for them, and re-layouts, gram_blocks(): real_half = split[:, :, :, 0].reshape(count_here, inputs_all, columns // 2)  32.4 us
    concatenate x1, local copies, waits for them, and re-layouts, on_device(): jnp.concatenate([real_part, imag_part], axis=2).astype(jnp.bfloat16)  28.6 us
    dot_general x2, matrix products, gram_blocks(): jnp.einsum('cik,cjk->cij', turned[:, first:last], turned[:, first:], pref...  25.1 us
    reshape x1, local copies, waits for them, and re-layouts, gram_blocks(): turned.reshape(count_here, inputs_all, columns // (2 * local_frame_count)...  23.7 us
  transfers between devices with their start and end apart: 3, of which 2 were waited for; matrix products, arithmetic and copies ran while one was open for 1% of the time, Pallas kernels for 0%

commit v1 on v0

--- a/solution.py
+++ b/solution.py
@@ -96,7 +96,19 @@
     local_flags = lax.dynamic_slice_in_dim(
         channel_flags, lax.axis_index("tm") * channels_here, channels_here, 0
     )
-    turned = lax.all_to_all(spectra, "feed", split_axis=0, concat_axis=1, tiled=True)
+    ways, here = (lax.axis_size("feed"), lax.axis_index("feed"))
+    width = spectra.shape[0] // ways
+    lengths = list(spectra.shape)
+    lengths[0] = width
+    height = lengths[1]
+    lengths[1] = height * ways
+    full = jnp.zeros(lengths, spectra.dtype)
+    for mask in range(ways):
+        part = lax.dynamic_slice_in_dim(spectra, (here ^ mask) * width, width, axis=0)
+        if mask:
+            part = lax.ppermute(part, "feed", [(d, d ^ mask) for d in range(ways)])
+        full = lax.dynamic_update_slice_in_dim(full, part, (here ^ mask) * height, axis=1)
+    turned = full
     visibility = lax.psum_scatter(
         gram_blocks(turned, local_frame_count, frame_total), "tm", scatter_dimension=0, tiled=True
     )

time: 799 us -> 816 us (1.021); the launches traced: 797 us -> 804 us
  waiting for transfers between devices: 462 us -> 408 us
  local copies, waits for them, and re-layouts: 139 us -> 175 us
  other arithmetic: 55.9 us -> 78.3 us
    all_to_all x1 -> x0, waiting for transfers between devices: 184 us -> none  [on_device(): lax.all_to_all(spectra, 'feed', split_axis=0, concat_axis=1, tiled=True)]
    ppermute x0 -> x7, waiting for transfers between devices: none -> 127 us  [on_device(): part = lax.ppermute(part, 'feed', [(d, d ^ mask) for d in range(ways)])]
    dynamic_slice x0 -> x8, local copies, waits for them, and re-layouts: none -> 43.6 us  [on_device(): lax.dynamic_slice_in_dim(spectra, (here ^ mask) * width, width, axis=0)]
    concatenate x1 -> x0, local copies, waits for them, and re-layouts: 28.6 us -> none  [on_device(): jnp.concatenate([real_part, imag_part], axis=2).astype(jnp.bfloat16)]
    dynamic_update_slice x0 -> x8, local copies, waits for them, and re-layouts: none -> 23.2 us  [on_device(): lax.dynamic_update_slice_in_dim(full, part, (here ^ mask) * height, axis=1)]
    concatenate x1 -> x2, other arithmetic: 6.52 us -> 21.8 us  [on_device(): jnp.concatenate([real_part, imag_part], axis=2).astype(jnp.bfloat16)]
    all_to_all x1 -> x0, local copies, waits for them, and re-layouts: 14.1 us -> none  [on_device(): lax.all_to_all(spectra, 'feed', split_axis=0, concat_axis=1, tiled=True)]
    unnamed x13 -> x19, local copies, waits for them, and re-layouts: 40.1 us -> 46 us
  transfers between devices with their start and end apart: 3 -> 9, of which waited for: 2 -> 4; matrix products, arithmetic and copies ran while one was open for 1% -> 10% of each run, Pallas kernels for 0% -> 0%
where the time goes in v1:
time: 816 us; the launch traced here: 804 us
  waiting for transfers between devices  408 us (50%)
  local copies, waits for them, and re-layouts  175 us (21%)
  matrix products  117 us (14%)
  other arithmetic  78.3 us (10%)
  between operations  14 us (2%)
  starting transfers between devices  12.4 us (2%)
    reduce_scatter x1, waiting for transfers between devices, on_device(): lax.psum_scatter(gram_blocks(turned, local_frame_count, frame_total), 'tm...  280 us
    ppermute x7, waiting for transfers between devices, on_device(): part = lax.ppermute(part, 'feed', [(d, d ^ mask) for d in range(ways)])  127 us
    dot_general x1, matrix products, on_device(): jnp.einsum('cpn,isn->cips', dft_table, filtered, preferred_element_type=j...  56.7 us
    unnamed x19, local copies, waits for them, and re-layouts  46 us
    dynamic_slice x8, local copies, waits for them, and re-layouts, on_device(): lax.dynamic_slice_in_dim(spectra, (here ^ mask) * width, width, axis=0)  43.6 us
    slice x1, local copies, waits for them, and re-layouts, gram_blocks(): real_half = split[:, :, :, 0].reshape(count_here, inputs_all, columns // 2)  32.4 us
    dot_general x2, matrix products, gram_blocks(): jnp.einsum('cik,cjk->cij', turned[:, first:last], turned[:, first:], pref...  25.2 us
    reshape x1, local copies, waits for them, and re-layouts, gram_blocks(): turned.reshape(count_here, inputs_all, columns // (2 * local_frame_count)...  23.8 us
  transfers between devices with their start and end apart: 9, of which 4 were waited for; matrix products, arithmetic and copies ran while one was open for 10% of the time, Pallas kernels for 0%

profile of v1, /device:TPU:0, one launch (start us, length us, event | category | flops | bytes accessed | tf_op | source)
XLA Modules:
  0.0 804.1 jit_solution(2741663918819949896)
XLA Ops:
  6.5 0.0 reduce-scatter.2.cloned.1.call-start
  6.5 15.4 %copy.31 = bf16[4,8,256,1024]{3,2,1,0:T(8,128)(2,1)S(1)} copy(bf16[4,8,256,1024]{3,1,2,0:T(8,128)(2,1)} %bitcast.59) | data formatting | bytes 33554432
  22.0 5.8 copy-done.4
  27.8 0.1 slice.79
  27.9 4.9 collective-permute-start
  32.9 8.5 %negate_convert_fusion = (bf16[512,1,1024]{2,0,1:T(8,128)(2,1)S(1)}, bf16[512,1,1024]{2,0,1:T(8,128)(2,1)S(1)}) fusion(), kind=kLoop, calls=%fused_computation.72 | loop fusion | flops 8912896 | bytes 2097152 | tf_op jit(solution)/shard_map/convert.3
  41.5 0.3 multiply_cosine_fusion
  41.8 0.0 copy-done.5
  41.8 0.0 collective-permute-done
  41.8 19.1 %maximum_convert_fusion = f32[32,259,1024]{2,1,0:T(8,128)} fusion(bf16[32,256,1024]{2,1,0:T(8,128)(2,1)} %bitcast.58, bf16[32,3,1024]{2,1,0:T(4,128)(2,1)S(1)} %collective-permute-done), kind=kLoop, calls=%fused_computation.24 | loop fusion | flops 33947648 | bytes 50921472 | tf_op jit(solution)/shard_map/convert_element_type | solution.py:76
  60.9 56.7 %fusion.10 = f32[512,32,2,256]{0,3,2,1:T(8,128)} fusion(f32[32,259,1024]{2,1,0:T(8,128)} %maximum_convert_fusion, f32[1024]{0:T(1024)S(1)} %bitcast.62, f32[1024]{0:T(1024)S(1)} %bitcast.63, f32[1024]{0:T(1024)S(1)} %bitcast.61, f32[1024]{0:T(1024)S(1)} %bitcast.60, bf16[512,1,1024]{2,0,1:T(8,128)(2,1)S(1)} %get-tuple-element.23, ...), kind=kOutput, calls=%fused_computation.35 | convolution fusion | flops 17251172352 | bytes 169885696 | tf_op jit(solution)/shard_map/cpn,isn->cips/dot_general | solution.py:85
  117.6 12.3 %multiply_convert_fusion = (bf16[512,32,256]{0,2,1:T(8,128)(2,1)S(1)}, bf16[512,32,256]{0,2,1:T(8,128)(2,1)S(1)}) fusion(f32[512,32,2,256]{0,3,2,1:T(8,128)} %fusion.10, f32[512,32]{0,1:T(8,128)S(1)} %get-tuple-element.22, f32[512,32]{0,1:T(8,128)S(1)} %get-tuple-element.21), kind=kLoop, calls=%fused_computation.30 | loop fusion | flops 41943040 | bytes 50462720 | tf_op jit(solution)/shard_map/convert.1
  129.9 14.0 %fusion.17 = (bf16[64,32,512]{0,2,1:T(8,128)(2,1)}, bf16[64,32,512]{0,2,1:T(8,128)(2,1)}, bf16[64,32,512]{0,2,1:T(8,128)(2,1)}, bf16[64,32,512]{0,2,1:T(8,128)(2...) fusion(s32[]{:T(128)S(6)} %select_n.93, bf16[512,32,256]{0,2,1:T(8,128)(2,1)S(1)} %get-tuple-element.6, ...), kind=kLoop, calls=%fused_computation.44 | loop fusion | flops 25165824 | bytes 29360152 | tf_op jit(solution)/shard_map/concatenate | solution.py:92
  144.0 5.7 copy.18
  149.6 0.0 collective-permute-start.1
  149.6 4.7 copy.19
  154.3 1.6 collective-permute-start.2
  155.9 5.7 copy.20
  161.6 0.3 collective-permute-start.3
  161.9 5.8 copy.21
  167.7 1.6 collective-permute-start.4
  169.3 7.8 fusion.24
  177.1 5.7 copy.22
  182.7 0.1 collective-permute-start.5
  182.8 5.7 copy.23
  188.5 0.0 collective-permute-done.1
  188.5 2.5 collective-permute-start.6
  191.0 5.7 copy.24
  196.7 6.2 collective-permute-done.2
  202.9 1.4 collective-permute-start.7
  204.4 0.1 iota_compare_fusion
  204.5 4.7 copy.17
  209.1 5.9 broadcast_in_dim.10
  215.1 1.4 constant_dynamic-update-slice_fusion.7
  216.5 3.1 constant_dynamic-update-slice_fusion.6
  219.6 3.1 constant_dynamic-update-slice_fusion.5
  222.7 24.4 %collective-permute-done.3 = bf16[64,32,512]{2,1,0:T(8,128)(2,1)} collective-permute-done((bf16[64,32,512]{2,1,0:T(8,128)(2,1)}, bf16[64,32,512]{2,1,0:T(8,128)(2,1)}, u32[]{:S(2)}, u32[]{:S(2)}) %collective-permute-start.3) | collective-permute-done | bytes 2097184 | tf_op jit(solution)/shard_map/ppermute | solution.py:109
  247.1 3.1 constant_dynamic-update-slice_fusion.4
  250.2 0.0 collective-permute-done.4
  250.2 3.1 constant_dynamic-update-slice_fusion.3
  253.3 96.7 %collective-permute-done.5 = bf16[64,32,512]{2,1,0:T(8,128)(2,1)} collective-permute-done((bf16[64,32,512]{2,1,0:T(8,128)(2,1)}, bf16[64,32,512]{2,1,0:T(8,128)(2,1)}, u32[]{:S(2)}, u32[]{:S(2)}) %collective-permute-start.5) | collective-permute-done | bytes 2097184 | tf_op jit(solution)/shard_map/ppermute | solution.py:109
  350.1 3.1 constant_dynamic-update-slice_fusion.2
  353.2 0.0 collective-permute-done.6
  353.2 3.1 constant_dynamic-update-slice_fusion.1
  356.3 0.0 collective-permute-done.7
  356.3 3.1 constant_dynamic-update-slice_fusion
  359.4 23.8 %reshape.150 = bf16[64,256,1,2,256]{4,3,1,0,2:T(2,128)(2,1)} reshape(bf16[64,256,512]{2,1,0:T(8,128)(2,1)} %constant_dynamic-update-slice_fusion) | data formatting | bytes 33554432 | tf_op jit(solution)/shard_map/reshape | solution.py:35
  383.2 32.4 %fusion.53 = (bf16[64,256,1,1,256]{4,3,1,0,2:T(2,128)(2,1)}, bf16[64,256,1,1,256]{4,3,1,0,2:T(2,128)(2,1)}) fusion(bf16[64,256,1,2,256]{4,3,1,0,2:T(2,128)(2,1)} %reshape.150), kind=kLoop, calls=%fused_computation.94 | loop fusion | bytes 33554432 | tf_op jit(solution)/shard_map/slice | solution.py:38
  415.6 8.9 %copy.34 = bf16[64,256,1,1,256]{4,1,0,3,2:T(8,128)(2,1)S(1)} copy(bf16[64,256,1,1,256]{4,3,1,0,2:T(2,128)(2,1)} %get-tuple-element.7) | data formatting | bytes 16777216
  424.6 11.9 %copy.35 = bf16[64,256,1,1,256]{4,1,0,3,2:T(8,128)(2,1)S(1)} copy(bf16[64,256,1,1,256]{4,3,1,0,2:T(2,128)(2,1)} %get-tuple-element.8) | data formatting | bytes 16777216
  436.5 0.0 copy-start.1
  436.5 3.2 copy-done.1
  439.8 3.2 fusion.29
  443.0 9.5 %fusion.25 = f32[64,128,256]{2,1,0:T(8,128)} fusion(bf16[64,256,256]{2,1,0:T(8,128)(2,1)} %bitcast.54, bf16[64,256,256]{2,1,0:T(8,128)(2,1)S(1)} %bitcast.50), kind=kOutput, calls=%fused_computation.52 | convolution fusion | flops 1073741824 | bytes 20971520 | tf_op jit(solution)/shard_map/cik,cjk->cij/dot_general | solution.py:57
  452.5 10.1 %fusion.13 = f32[64,128,128]{2,1,0:T(8,128)} fusion(bf16[64,256,512]{2,1,0:T(8,128)(2,1)} %constant_dynamic-update-slice_fusion), kind=kOutput, calls=%fused_computation.36 | convolution fusion | flops 1073741824 | bytes 12582912 | tf_op jit(solution)/shard_map/cik,cjk->cij/dot_general | solution.py:45
  462.7 7.9 fusion.45
  470.6 15.0 %pad_select_fusion = f32[64,128,256]{2,1,0:T(8,128)} fusion(f32[64,128,128]{2,1,0:T(8,128)} %fusion.45, pred[128,256]{1,0:T(8,128)(4,1)S(1)} %iota_compare_fusion.1, bf16[64,256,512]{2,1,0:T(8,128)(2,1)} %constant_dynamic-update-slice_fusion), kind=kOutput, calls=%fused_computation.43 | convolution fusion | flops 2149580800 | bytes 37781504 | tf_op jit(solution)/shard_map/cik,cjk->cij/dot_general | solution.py:45
  485.6 14.3 %subtract_select_fusion = f32[64,128,256]{2,1,0:T(8,128)} fusion(f32[64,128,256]{2,1,0:T(8,128)} %fusion.25, f32[64,128,128]{2,1,0:T(8,128)} %fusion.13, pred[128,256]{1,0:T(8,128)(4,1)S(1)} %iota_compare_fusion, bf16[64,256,256]{2,1,0:T(8,128)(2,1)} %bitcast.52, bf16[64,256,256]{2,1,0:T(8,128)(2,1)} %bitcast.56), kind=kOutput, calls=%fused_computation.42 | convolution fusion | flops 1077936128 | bytes 33587200 | tf_op jit(solution)/shard_map/cik,cjk->cij/dot_general | solution.py:51
  499.8 11.4 %maximum_multiply_fusion = f32[64,256,256]{2,1,0:T(8,128)} fusion(f32[64,128,256]{2,1,0:T(8,128)} %subtract_select_fusion, f32[64,128,256]{2,1,0:T(8,128)} %pad_select_fusion), kind=kLoop, calls=%fused_computation.27 | loop fusion | flops 8388608 | bytes 33554432 | tf_op jit(solution)/shard_map/div | solution.py:67
  511.3 0.0 reduce-scatter.2.cloned.1.call-update
  511.3 0.6 copy-done.7
  511.9 0.1 dynamic-slice_convert_fusion
  512.0 280.1 %reduce-scatter.2.cloned.1.call-done = f32[16,256,256]{2,1,0:T(8,128)} async-done(((f32[64,256,256]{2,1,0:T(8,128)}), f32[16,256,256]{2,1,0:T(8,128)}) %reduce-scatter.2.cloned.1.call-update) | async-done | bytes 4194320 | tf_op jit(solution)/shard_map/reduce_scatter | solution.py:112
  792.2 4.7 broadcast_multiply_fusion
  (15 shorter events, 0.1 us)
Async XLA Ops:
  6.5 785.6 %reduce-scatter.2.cloned.1.call-start = ((), (), s32[]{:S(2)}) async-start(), calls=%async_computation.1 | async-start | bytes 20971520 | tf_op jit(solution)/shard_map/reduce_scatter | solution.py:112
  6.5 34.9 %copy-start.6 = (f32[32]{0:T(128)S(1)}, f32[32]{0:T(128)}, u32[]{:S(2)}) copy-start(f32[32]{0:T(128)} %param.6) | copy-start | bytes 388
  6.5 35.2 %copy-start.5 = (f32[4,1024]{1,0:T(4,128)S(1)}, f32[4,1024]{1,0:T(4,128)}, u32[]{:S(2)}) copy-start(f32[4,1024]{1,0:T(4,128)} %param.5) | copy-start | bytes 49156
  21.9 5.8 copy-start.4
  27.9 13.9 %collective-permute-start = (bf16[32,3,1024]{2,1,0:T(4,128)(2,1)S(1)}, bf16[32,3,1024]{2,1,0:T(4,128)(2,1)S(1)}, u32[]{:S(2)}, u32[]{:S(2)}) collective-permute-start(bf16[32,3,1024]{2,1,0:T(4,128)(2,1)S(1)} %slice.79), channel_id=1, source_target_pairs={{0,1},{1,2},{2,3},{4,5},{5,6},{6,7},{8,9},{9,10},{10,11},{12,13},{... | collective-permute-start | bytes 589832 | tf_op jit(solution)/shard_map/ppermute | solution.py:11
  129.9 14.0 %copy-start.2 = (bf16[512,32,256]{0,2,1:T(8,128)(2,1)}, bf16[512,32,256]{0,2,1:T(8,128)(2,1)S(1)}, u32[]{:S(2)}) copy-start(bf16[512,32,256]{0,2,1:T(8,128)(2,1)S(1)} %get-tuple-element.5) | copy-start | bytes 25165828
  129.9 14.0 %copy-start.3 = (bf16[512,32,256]{0,2,1:T(8,128)(2,1)}, bf16[512,32,256]{0,2,1:T(8,128)(2,1)S(1)}, u32[]{:S(2)}) copy-start(bf16[512,32,256]{0,2,1:T(8,128)(2,1)S(1)} %get-tuple-element.6) | copy-start | bytes 25165828
  149.6 38.9 %collective-permute-start.1 = (bf16[64,32,512]{2,1,0:T(8,128)(2,1)}, bf16[64,32,512]{2,1,0:T(8,128)(2,1)}, u32[]{:S(2)}, u32[]{:S(2)}) collective-permute-start(bf16[64,32,512]{2,1,0:T(8,128)(2,1)} %copy.18), channel_id=1, source_target_pairs={{0,4},{4,0},{8,12},{12,8},{16,20},{20,16},{24,28},{28,24},{1,5},{5... | collective-permute-start | bytes 6291464 | tf_op jit(solution)/shard_map/ppermute | solution.py:109
  154.3 48.6 %collective-permute-start.2 = (bf16[64,32,512]{2,1,0:T(8,128)(2,1)S(1)}, bf16[64,32,512]{2,1,0:T(8,128)(2,1)}, u32[]{:S(2)}, u32[]{:S(2)}) collective-permute-start(bf16[64,32,512]{2,1,0:T(8,128)(2,1)S(1)} %copy.19), channel_id=1, source_target_pairs={{0,8},{4,12},{8,0},{12,4},{16,24},{20,28},{24,16},{28,20},{1,9},{5... | collective-permute-start | bytes 6291464 | tf_op jit(solution)/shard_map/ppermute | solution.py:109
  161.6 85.5 %collective-permute-start.3 = (bf16[64,32,512]{2,1,0:T(8,128)(2,1)}, bf16[64,32,512]{2,1,0:T(8,128)(2,1)}, u32[]{:S(2)}, u32[]{:S(2)}) collective-permute-start(bf16[64,32,512]{2,1,0:T(8,128)(2,1)} %copy.20), channel_id=1, source_target_pairs={{0,12},{4,8},{8,4},{12,0},{16,28},{20,24},{24,20},{28,16},{1,13},{... | collective-permute-start | bytes 6291464 | tf_op jit(solution)/shard_map/ppermute | solution.py:109
  167.7 82.4 %collective-permute-start.4 = (bf16[64,32,512]{2,1,0:T(8,128)(2,1)}, bf16[64,32,512]{2,1,0:T(8,128)(2,1)}, u32[]{:S(2)}, u32[]{:S(2)}) collective-permute-start(bf16[64,32,512]{2,1,0:T(8,128)(2,1)} %copy.21), channel_id=1, source_target_pairs={{0,16},{4,20},{8,24},{12,28},{16,0},{20,4},{24,8},{28,12},{1,17},{... | collective-permute-start | bytes 6291464 | tf_op jit(solution)/shard_map/ppermute | solution.py:109
  182.7 167.3 %collective-permute-start.5 = (bf16[64,32,512]{2,1,0:T(8,128)(2,1)}, bf16[64,32,512]{2,1,0:T(8,128)(2,1)}, u32[]{:S(2)}, u32[]{:S(2)}) collective-permute-start(bf16[64,32,512]{2,1,0:T(8,128)(2,1)} %copy.22), channel_id=1, source_target_pairs={{0,20},{4,16},{8,28},{12,24},{16,4},{20,0},{24,12},{28,8},{1,21},{... | collective-permute-start | bytes 6291464 | tf_op jit(solution)/shard_map/ppermute | solution.py:109
  188.5 164.7 %collective-permute-start.6 = (bf16[64,32,512]{2,1,0:T(8,128)(2,1)}, bf16[64,32,512]{2,1,0:T(8,128)(2,1)}, u32[]{:S(2)}, u32[]{:S(2)}) collective-permute-start(bf16[64,32,512]{2,1,0:T(8,128)(2,1)} %copy.23), channel_id=1, source_target_pairs={{0,24},{4,28},{8,16},{12,20},{16,8},{20,12},{24,0},{28,4},{1,25},{... | collective-permute-start | bytes 6291464 | tf_op jit(solution)/shard_map/ppermute | solution.py:109
  202.9 153.4 %collective-permute-start.7 = (bf16[64,32,512]{2,1,0:T(8,128)(2,1)}, bf16[64,32,512]{2,1,0:T(8,128)(2,1)}, u32[]{:S(2)}, u32[]{:S(2)}) collective-permute-start(bf16[64,32,512]{2,1,0:T(8,128)(2,1)} %copy.24), channel_id=1, source_target_pairs={{0,28},{4,24},{8,20},{12,16},{16,12},{20,8},{24,4},{28,0},{1,29},{... | collective-permute-start | bytes 6291464 | tf_op jit(solution)/shard_map/ppermute | solution.py:109
  424.6 18.4 %copy-start = (bf16[64,256,1,1,256]{4,1,0,3,2:T(8,128)(2,1)}, bf16[64,256,1,1,256]{4,1,0,3,2:T(8,128)(2,1)S(1)}, u32[]{:S(2)}) copy-start(bf16[64,256,1,1,256]{4,1,0,3,2:T(8,128)(2,1)S(1)} %copy.34) | copy-start | bytes 25165828
  436.5 3.3 copy-start.1
  511.3 0.7 copy-start.7
Sparse Core Ops, SparseCore 0:
  511.4 280.6 reduce-scatter.1
